TPU v7x, 32 devices: a whole 2x2x4 slice. The times are simulated.
32 devices in a mesh: ma: 8 (over z, y), sa: 4 (over x, core).
Axes of the slice: x: 2, y: 2, z: 4, core: 2. Of those that a mesh axis runs over, the one named last changes fastest.
Arguments:
- initial_heat_matrix: float32 [128, 128, 8192], P('ma', 'sa'), may hold values from -6 to 6
- conductivity: float32 [128, 8192], P('sa'), may hold values from 0.5 to 2
- laser_x: int32 [128, 2], P('ma'), may hold values from 0 to 127
- laser_y: int32 [128, 2], P('ma'), may hold values from 0 to 127
- pixel_cell: int32 [128, 512], P('sa', 'ma'), may hold values from 0 to 127, as said below
- observed: float32 [128, 512], P('sa', 'ma'), may hold values from -6 to 6
- obs_var: float32 [128, 512], P('sa', 'ma'), may hold values from 20 to 400
Outputs:
- analysis: float32 [128, 128, 8192], P('ma', 'sa')
Inputs may be any that keep to these rules, and one draw needn't show every extreme that they name: `pixel_cell`: pixel column j views a surface cell y of its own plane; y lies within 2 of j // 4 and in the same aligned group of 16 cells as that value.
All inputs are finite; a program needn't handle non-finite values.
Results may differ from a plain program's by a relative error of at most 0.000096.
Values sent between devices are 32-bit elements; how exact they have to be, the bound alone decides.
A program may use at most 384 MiB of HBM per device.

v0:
```python
import jax
import jax.numpy as jnp
from jax import lax
from jax.sharding import PartitionSpec as P

CELLS_DEPTHWISE = 64


step_dt = 0.025
alpha_cond = 0.05
laser_power = 12.0
beam_spot_width = 18.0


def extended(block, sides, width):
    for axis, dim in sides:
        count = lax.axis_size(axis)
        forward = [(i, i + 1) for i in range(count - 1)]
        backward = [(target, source) for source, target in forward]
        low = lax.ppermute(
            lax.slice_in_dim(block, block.shape[dim] - width, None, axis=dim), axis, forward
        )
        high = lax.ppermute(lax.slice_in_dim(block, 0, width, axis=dim), axis, backward)
        block = jnp.concatenate([low, block, high], axis=dim)
    return block


def conduct(field_ext, cond_ext, first_plane, spot_x, spot_y):
    kext = cond_ext[None] * (1.0 + alpha_cond * field_ext * field_ext)
    fpad = jnp.pad(field_ext, ((0, 0), (0, 0), (1, 1), (1, 1)))
    kpad = jnp.pad(kext, ((0, 0), (0, 0), (1, 1), (1, 1)))
    centre = fpad[:, 1:-1, 1:-1, 1:-1]
    kcentre = kpad[:, 1:-1, 1:-1, 1:-1]
    shifted = [
        (slice(2, None), slice(1, -1), slice(1, -1)),
        (slice(None, -2), slice(1, -1), slice(1, -1)),
        (slice(1, -1), slice(2, None), slice(1, -1)),
        (slice(1, -1), slice(None, -2), slice(1, -1)),
        (slice(1, -1), slice(1, -1), slice(2, None)),
        (slice(1, -1), slice(1, -1), slice(None, -2)),
    ]
    flux = jnp.zeros_like(centre)
    for pick in shifted:
        neighbour = fpad[(slice(None),) + pick]
        kneigh = kpad[(slice(None),) + pick]
        flux = flux + 0.5 * (kcentre + kneigh) * (neighbour - centre)
    width = centre.shape[1]
    rows_y = centre.shape[2]
    depth = centre.shape[3]
    xglob = first_plane + jnp.arange(width, dtype=jnp.int32)
    yglob = jnp.arange(rows_y, dtype=jnp.int32)
    delta_x = (xglob[None, :] - spot_x[:, None]).astype(jnp.float32)
    delta_y = (yglob[None, :] - spot_y[:, None]).astype(jnp.float32)
    spot = laser_power * jnp.exp(
        -(delta_x[:, :, None] ** 2 + delta_y[:, None, :] ** 2) / beam_spot_width
    )
    surface_top = (jnp.arange(depth, dtype=jnp.int32) == depth - 1).astype(jnp.float32)
    heat = spot[:, :, :, None] * surface_top[None, None, None, :]
    return centre + step_dt * (flux + heat)


def transform(block, mix):
    fmean = jnp.mean(block, axis=0)
    anom = block - fmean[None]
    return fmean[None] + jnp.einsum("jxc,jk->kxc", anom, mix, precision=lax.Precision.HIGHEST)


def lower_factor(amat):
    count = amat.shape[0]
    positions = jnp.arange(count, dtype=jnp.int32)

    def column_step(index_j, factor):
        row_j = lax.dynamic_slice_in_dim(factor, index_j, 1, 0)[0]
        row_j = jnp.where(positions < index_j, row_j, 0.0)
        column = lax.dynamic_slice_in_dim(amat, index_j, 1, 1)[:, 0]
        rest = column - jnp.dot(factor, row_j, precision=lax.Precision.HIGHEST)
        pivot = jnp.sqrt(lax.dynamic_slice_in_dim(rest, index_j, 1, 0)[0])
        fresh = jnp.where(
            positions > index_j, rest / pivot, jnp.where(positions == index_j, pivot, 0.0)
        )
        return jnp.where((positions == index_j)[None, :], fresh[:, None], factor)

    return lax.fori_loop(0, count, column_step, jnp.zeros_like(amat))


def lower_inverse(factor):
    count = factor.shape[0]
    positions = jnp.arange(count, dtype=jnp.int32)

    def row_step(index_i, inverse):
        row_i = lax.dynamic_slice_in_dim(factor, index_i, 1, 0)[0]
        pivot = lax.dynamic_slice_in_dim(row_i, index_i, 1, 0)[0]
        unit = (positions == index_i).astype(jnp.float32)
        fresh = (unit - jnp.dot(row_i, inverse, precision=lax.Precision.HIGHEST)) / pivot
        return jnp.where((positions == index_i)[:, None], fresh[None, :], inverse)

    return lax.fori_loop(0, count, row_step, jnp.zeros_like(factor))


def per_device(initial_heat_matrix, conductivity, laser_x, laser_y, pixel_cell, observed, obs_var):
    members, planes, columns = initial_heat_matrix.shape
    depth = CELLS_DEPTHWISE
    rows_y = columns // depth
    first = lax.axis_index("sa") * planes
    total_planes = planes * lax.axis_size("sa")
    field = initial_heat_matrix.reshape(members, planes, rows_y, depth)
    cond_grid = conductivity.reshape(1, planes, rows_y, depth)
    stacked = jnp.concatenate([field, cond_grid], axis=0)
    wider = extended(stacked, (("sa", 1),), 2)
    cond_wide = wider[members]
    middle = conduct(wider[:members], cond_wide, first - 1, laser_x[:, 0], laser_y[:, 0])
    plane_ids = first - 1 + jnp.arange(planes + 2, dtype=jnp.int32)
    inside = ((plane_ids >= 0) & (plane_ids < total_planes)).astype(jnp.float32)
    middle = middle * inside[None, :, None, None]
    field = conduct(middle, cond_wide[1:-1], first, laser_x[:, 1], laser_y[:, 1])
    member_states = field.reshape(members, planes, columns)
    gathered = lax.all_to_all(member_states, "ma", split_axis=2, concat_axis=0, tiled=True)
    total_members = gathered.shape[0]
    group_rows = gathered.shape[2] // depth
    surface = gathered.reshape(total_members, planes, group_rows, depth)[:, :, :, depth - 1]
    group_rows = surface.shape[2]
    local_rows = pixel_cell % group_rows
    onehot = (
        local_rows[:, None, :] == jnp.arange(group_rows, dtype=jnp.int32)[None, :, None]
    ).astype(jnp.float32)
    seen = jnp.einsum("kxy,xyj->kxj", surface, onehot, precision=lax.Precision.HIGHEST)
    seen_mean = jnp.mean(seen, axis=0)
    seen_anom = seen - seen_mean[None]
    innovation = observed - seen_mean
    weight = 1.0 / obs_var
    gram_part = jnp.einsum(
        "kxj,lxj->kl", seen_anom * weight[None], seen_anom, precision=lax.Precision.HIGHEST
    )
    proj_part = jnp.einsum(
        "kxj,xj->k", seen_anom, weight * innovation, precision=lax.Precision.HIGHEST
    )
    gram, proj = lax.psum((gram_part, proj_part), ("ma", "sa"))
    count = gram.shape[0]
    eye = jnp.eye(count, dtype=jnp.float32)
    amat = eye + gram / (count - 1)
    factor = lower_factor(amat)
    inverse = lower_inverse(factor)
    wroot = inverse.T
    middle_sol = jnp.dot(inverse, proj, precision=lax.Precision.HIGHEST)
    wmean = jnp.dot(wroot, middle_sol, precision=lax.Precision.HIGHEST) / (count - 1)
    mix = wroot + wmean[:, None]
    done = transform(gathered, mix)
    return lax.all_to_all(done, "ma", split_axis=0, concat_axis=2, tiled=True)


def solution(mesh):
    placed = (
        P("ma", "sa", None),
        P("sa", None),
        P("ma", None),
        P("ma", None),
        P("sa", "ma"),
        P("sa", "ma"),
        P("sa", "ma"),
    )
    return jax.shard_map(
        per_device, mesh=mesh, in_specs=placed, out_specs=P("ma", "sa", None), check_vma=False
    )
```

profile of v0, /device:TPU:0, one launch (start us, length us, event | category | flops | bytes accessed | tf_op | source)
XLA Modules:
  0.0 2191.7 jit_solution(17658031716975416276)
XLA Ops:
  6.5 27.0 %reshape.177 = f32[16,32,128,64]{3,2,1,0:T(8,128)} reshape(f32[16,32,8192]{2,1,0:T(8,128)} %param.11) | data formatting | bytes 33554432 | tf_op jit(solution)/shard_map/reshape | solution.py:106
  33.5 23.3 %constant_dynamic-update-slice_fusion.1 = f32[17,32,128,64]{3,2,1,0:T(8,128)} fusion(f32[16,32,128,64]{3,2,1,0:T(8,128)} %reshape.177), kind=kLoop, calls=%fused_computation.160 | loop fusion | bytes 50331648
  59.1 4.1 fusion.104
  66.0 3.4 collective-permute-start
  80.1 26.2 %pad_maximum_fusion = f32[17,36,128,64]{3,2,1,0:T(8,128)} fusion(f32[17,2,128,64]{3,2,1,0:T(8,128)} %copy.18, f32[17,32,128,64]{3,2,1,0:T(8,128)} %constant_dynamic-update-slice_fusion, f32[17,2,128,64]{3,2,1,0:T(8,128)S(1)} %copy.17), kind=kLoop, calls=%fused_computation.30 | loop fusion | flops 10027008 | bytes 40108032 | tf_op jit(solution)/shard_map/concatenate | solution.py:24
  106.3 3.5 maximum_bitcast_fusion
  113.0 36.7 %fusion.23 = (f32[16,36,128,64]{3,2,1,0:T(8,128)}, f32[16,36,128,64]{3,2,1,0:T(8,128)}) fusion(f32[36,128,64]{2,1,0:T(8,128)} %maximum_bitcast_fusion, f32[17,36,128,64]{3,2,1,0:T(8,128)} %pad_maximum_fusion), kind=kLoop, calls=%fused_computation.32 | loop fusion | flops 18874368 | bytes 57802752 | tf_op jit(solution)/shard_map/mul | solution.py:29
  149.7 179.5 %fusion.49 = (f32[16,34,128,64]{3,2,1,0:T(8,128)}, f32[16,34,128,64]{3,2,1,0:T(8,128)}) fusion(f32[34,128,64]{2,1,0:T(8,128)} %maximum_bitcast_fusion.1, f32[34]{0:T(128)S(1)} %and_convert_fusion, f32[64]{0:T(128)S(1)} %compare_convert_fusion, f32[16,34,128]{2,1,0:T(8,128)S(1)} %exponential_multiply_fusion, f32[16,36,128,64]{3,2,1,0:T(8,128)} %get-tuple-element.281, ...), kind=kLoop, calls=%fused_computation.66 | loop fusion | flops 178257920 | bytes 295256448 | tf_op jit(solution)/shard_map/mul | solution.py:29
  329.2 165.0 %fusion.66 = f32[16,32,128,64]{3,2,1,0:T(8,128)} fusion(f32[16,34,128,64]{3,2,1,0:T(8,128)} %get-tuple-element.278, f32[16,34,128,64]{3,2,1,0:T(8,128)} %get-tuple-element.279, f32[64]{0:T(128)S(1)} %compare_convert_fusion, f32[16,32,128]{2,1,0:T(8,128)S(1)} %copy-done.4), kind=kLoop, calls=%fused_computation.95 | loop fusion | flops 138412032 | bytes 289669376 | tf_op jit(solution)/shard_map/add | solution.py:59
  494.2 45.2 %copy.30 = f32[16,32,128,64]{1,0,3,2:T(8,128)} copy(f32[16,32,128,64]{3,2,1,0:T(8,128)} %fusion.66) | data formatting | bytes 33554432 | tf_op jit(solution)/shard_map/reshape | solution.py:116
  539.4 67.4 %reshape.193 = f32[8,1,524288]{2,1,0:T(1,128)} reshape(f32[8192,16,32]{2,1,0:T(8,128)} %bitcast.86) | data formatting | bytes 33554432
  606.7 6.0 all-to-all-start
  612.8 353.2 %all-to-all-done = f32[8,1,524288]{2,1,0:T(1,128)} async-done(((f32[8,1,524288]{2,1,0:T(1,128)}), f32[8,1,524288]{2,1,0:T(1,128)}, u32[]{:S(2)}, u32[]{:S(2)}) %all-to-all-start) | async-done | bytes 16777248 | tf_op jit(solution)/shard_map/all_to_all | solution.py:117
  966.6 50.5 %reduce.1 = f32[8,524288]{1,0:T(8,128)} reduce(f32[8,1,524288]{2,1,0:T(1,128)} %all-to-all-done, f32[]{:T(128)} %broadcast.207), dimensions={1}, to_apply=%all_to_all.26.reduce_sub_computation | reduce | bytes 33554436 | tf_op jit(solution)/shard_map/all_to_all | solution.py:117
  1017.1 55.4 %reshape.194 = f32[8192,16,32]{2,1,0:T(8,128)} reshape(f32[8,524288]{1,0:T(8,128)} %reduce.1) | data formatting | bytes 33554432
  1072.5 42.5 %copy.23 = f32[8,16,32,1024]{3,2,1,0:T(8,128)} copy(f32[8,16,32,1024]{2,1,3,0:T(8,128)} %bitcast.9) | data formatting | bytes 33554432 | tf_op jit(solution)/shard_map/all_to_all | solution.py:117
  1114.9 44.4 %copy.26 = f32[8,16,32,1024]{3,1,0,2:T(8,128)} copy(f32[8,16,32,1024]{2,1,3,0:T(8,128)} %bitcast.9) | data formatting | bytes 33554432 | tf_op jit(solution)/shard_map/all_to_all | solution.py:117
  1159.3 25.8 %reshape.180 = f32[128,32,16,64]{3,2,1,0:T(8,128)} reshape(f32[8,16,32,1024]{3,2,1,0:T(8,128)} %copy.23) | data formatting | bytes 33554432 | tf_op jit(solution)/shard_map/reshape | solution.py:120
  1185.1 25.2 %slice.190 = f32[128,32,16,1]{3,2,1,0:T(8,128)} slice(f32[128,32,16,64]{3,2,1,0:T(8,128)} %reshape.180), slice={[0:128], [0:32], [0:16], [63:64]} | slice | bytes 524288 | tf_op jit(solution)/shard_map/slice | solution.py:120
  1210.3 19.1 copy.34
  1230.6 3.3 fusion.87
  1233.9 34.8 %copy.31 = f32[16,32,8,1024]{3,2,1,0:T(8,128)} copy(f32[16,32,8,1024]{1,0,3,2:T(8,128)} %bitcast.7) | data formatting | bytes 33554432 | tf_op jit(solution)/shard_map/all_to_all | solution.py:117
  1268.7 7.9 bitcast_reduce_fusion
  1276.7 12.3 bitcast_subtract_fusion
  1289.8 48.9 %psum.15 = f32[128]{0:T(128)S(1)} all-reduce(f32[128]{0:T(128)S(1)} %convolution_bitcast_fusion.3), channel_id=1, replica_groups=mesh['ma'=8,'sa'=4] {'ma','sa'}, use_global_device_ids=true, to_apply=%region_7.8 | all-reduce | flops 128 | bytes 1024 | tf_op jit(solution)/shard_map/psum | solution.py:137
  1338.7 24.4 %all-reduce.6.cloned.1.call-done = f32[128,128]{1,0:T(8,128)} async-done(((f32[128,128]{1,0:T(8,128)}), f32[128,128]{1,0:T(8,128)}) %all-reduce.6.cloned.1.call-update) | async-done | bytes 65552 | tf_op jit(solution)/shard_map/psum | solution.py:137
  1364.0 212.1 %while.33 = (s32[]{:T(128)}, f32[128,128]{1,0:T(8,128)S(1)}, f32[128,128]{0,1:T(8,128)S(1)}, s32[]{:T(128)}, s32[]{:T(128)}) while((s32[]{:T(128)}, f32[128,128]{1,0:T(8,128)S(1)}, f32[128,128]{0,1:T(8,128)S(1)}, s32[]{:T(128)}, s32[]{:T(128)}) %tuple.94), condition=%wide.region_4.5_spmd.clone.clone, body=%wide.region_3.4_spmd.clone.clone.sunk | while | flops 246915 | bytes 332648 | solution.py:83
  1576.2 195.6 %while.32 = (s32[]{:T(128)}, f32[128,128]{1,0:T(8,128)S(1)}, f32[128,128]{1,0:T(8,128)S(1)}, s32[]{:T(128)}, s32[]{:T(128)}, /*index=5*/s32[]{:T(128)}) while((s32[]{:T(128)}, f32[128,128]{1,0:T(8,128)S(1)}, f32[128,128]{1,0:T(8,128)S(1)}, s32[]{:T(128)}, s32[]{:T(128)}, /*index=5*/s32[]{:T(128)}) %tuple.93), condition=%wide.region_6.7_spmd.clone, body=%wide.region_5.6_spmd.clone.sunk | while | flops 246404 | bytes 200048 | solution.py:97
  1772.2 21.8 convolution_add_fusion
  1794.0 15.7 copy.27
  1809.6 368.8 %all_to_all.36 = f32[128,32,1024]{2,1,0:T(8,128)S(1)} all-to-all(f32[128,32,1024]{2,1,0:T(8,128)S(1)} %copy.27), channel_id=1, replica_groups=mesh['ma'=8,'sa'=4] {'ma'}, dimensions={0} | all-to-all | bytes 33554432 | tf_op jit(solution)/shard_map/all_to_all | solution.py:148
  2178.5 6.2 copy.35
  (1335 shorter events, 331.4 us)
Async XLA Ops:
  33.5 23.3 %copy-start.3 = (f32[32,8192]{1,0:T(8,128)S(1)}, f32[32,8192]{1,0:T(8,128)}, u32[]{:S(2)}) copy-start(f32[32,8192]{1,0:T(8,128)} %param.12) | copy-start | bytes 3145732
  33.5 39.2 %copy-start.8 = (s32[16,2]{0,1:T(2,128)S(1)}, s32[16,2]{0,1:T(2,128)}, u32[]{:S(2)}) copy-start(s32[16,2]{0,1:T(2,128)} %param.13) | copy-start | bytes 388
  33.5 39.3 %copy-start.9 = (s32[16,2]{0,1:T(2,128)S(1)}, s32[16,2]{0,1:T(2,128)}, u32[]{:S(2)}) copy-start(s32[16,2]{0,1:T(2,128)} %param.14) | copy-start | bytes 388
  66.0 8.0 collective-permute-start
  71.1 6.1 collective-permute-start.1
  106.3 3.5 copy-start
  149.7 179.5 %copy-start.4 = (f32[16,32,128]{2,1,0:T(8,128)S(1)}, f32[16,32,128]{2,1,0:T(8,128)}, u32[]{:S(2)}) copy-start(f32[16,32,128]{2,1,0:T(8,128)} %exponential_multiply_fusion.1) | copy-start | bytes 786436
  606.7 6.0 copy-start.5
  606.7 359.3 %all-to-all-start = ((f32[8,1,524288]{2,1,0:T(1,128)}), f32[8,1,524288]{2,1,0:T(1,128)}, u32[]{:S(2)}, u32[]{:S(2)}) async-start(f32[8,1,524288]{2,1,0:T(1,128)} %reshape.193), calls=%async_computation | async-start | bytes 33554432 | tf_op jit(solution)/shard_map/all_to_all | solution.py:117
  612.7 750.4 %all-reduce.6.cloned.1.call-start = ((), (), s32[]{:S(2)}) async-start(), calls=%async_computation.2 | async-start | bytes 131072 | tf_op jit(solution)/shard_map/psum | solution.py:137
  1210.3 20.3 copy-start.6
  1210.3 20.3 copy-start.7
  1268.7 95.3 %copy-start.2 = (f32[128,128]{1,0:T(8,128)S(1)}, f32[128,128]{1,0:T(8,128)}, u32[]{:S(2)}) copy-start(f32[128,128]{1,0:T(8,128)} %custom-call.1) | copy-start | bytes 196612
  1268.7 307.5 %copy-start.1 = (f32[128,128]{1,0:T(8,128)S(1)}, f32[128,128]{1,0:T(8,128)}, u32[]{:S(2)}) copy-start(f32[128,128]{1,0:T(8,128)} %custom-call) | copy-start | bytes 196612
Sparse Core Ops, SparseCore 0:
  1234.1 128.9 all-reduce.5
where the time goes:
time: 2200 us; the launch traced here: 2190 us
  local copies, waits for them, and re-layouts  605 us (28%)
  other arithmetic  514 us (23%)
  blocking collectives  418 us (19%)
  waiting for transfers between devices  379 us (17%)
  matrix products  152 us (7%)
  loops' own time  99.2 us (5%)
    all_to_all x1, blocking collectives, per_device(): return lax.all_to_all(done, 'ma', split_axis=0, concat_axis=2, tiled=True)  369 us
    all_to_all x1, waiting for transfers between devices, per_device(): lax.all_to_all(member_states, 'ma', split_axis=2, concat_axis=0, tiled=True)  353 us
    mul x4, other arithmetic, conduct(): kext = cond_ext[None] * (1.0 + alpha_cond * field_ext * field_ext)  223 us
    unnamed x25, local copies, waits for them, and re-layouts  165 us
    add x1, other arithmetic, conduct(): return centre + step_dt * (flux + heat)  165 us
    all_to_all x4, local copies, waits for them, and re-layouts, per_device(): lax.all_to_all(member_states, 'ma', split_axis=2, concat_axis=0, tiled=True)  122 us
    dot_general x128, matrix products, row_step(): jnp.dot(row_i, inverse, precision=lax.Precision.HIGHEST)  102 us
    another operation x1, loops' own time, lower_factor(): return lax.fori_loop(0, count, column_step, jnp.zeros_like(amat))  94.8 us
  transfers between devices with their start and end apart: 4, of which 3 were waited for; matrix products, arithmetic and copies ran while one was open for 3% of the time, Pallas kernels for 0%

commit v1 on v0

v1 whole, which is shorter than its diff:
```python
import jax
import jax.numpy as jnp
from jax import lax
from jax.experimental import pallas as pl
from jax.experimental.pallas import tpu as pltpu
from jax.sharding import PartitionSpec as P

CELLS_DEPTHWISE = 64


step_dt = 0.025
alpha_cond = 0.05
laser_power = 12.0
beam_spot_width = 18.0


def halo(block, axis, width):
    count = lax.axis_size(axis)
    forward = [(i, i + 1) for i in range(count - 1)]
    backward = [(target, source) for source, target in forward]
    dim = block.ndim - 2
    low = lax.ppermute(
        lax.slice_in_dim(block, block.shape[dim] - width, None, axis=dim), axis, forward
    )
    high = lax.ppermute(lax.slice_in_dim(block, 0, width, axis=dim), axis, backward)
    return low, high


def forecast_kernel(
    depth, planes, wide, total_planes, first_ref, lx_ref, ly_ref, u_ref, low_ref, high_ref,
    cond_ref, out_ref, ustart, umid
):
    member = pl.program_id(0)
    rows = ustart.shape[0]
    parts, _, _, per_part = out_ref.shape
    columns = parts * per_part
    edge = 128
    ustart[2 : 2 + planes, edge : edge + columns] = u_ref[0]
    ustart[0:2, edge : edge + columns] = low_ref[0]
    ustart[2 + planes : 4 + planes, edge : edge + columns] = high_ref[0]
    ustart[4 + planes : rows, edge : edge + columns] = jnp.zeros(
        (rows - 4 - planes, columns), jnp.float32
    )
    for buf in (ustart, umid):
        buf[:, 0:edge] = jnp.zeros((rows, edge), jnp.float32)
        buf[:, edge + columns :] = jnp.zeros((rows, edge), jnp.float32)
    xpos = first_ref[0] - 2 + lax.broadcasted_iota(jnp.int32, (rows, 1), 0)
    inside = jnp.where((xpos >= 0) & (xpos < total_planes), 1.0, 0.0)
    lane = lax.broadcasted_iota(jnp.int32, (1, wide), 1)
    zpos = lane % depth
    top = zpos == depth - 1
    bottom = zpos == 0
    span = wide + 2 * edge

    def advance(source, start, step):
        ext = source[:, pl.ds(start, span)]
        kext = cond_ref[:, pl.ds(start, span)] * (1.0 + alpha_cond * ext * ext)
        centre = ext[:, edge : edge + wide]
        kcentre = kext[:, edge : edge + wide]

        def lanes(value, shift):
            return pltpu.roll(value, shift % span, 1)[:, edge : edge + wide]

        def face(neighbour, kneigh):
            return (kcentre + kneigh) * (neighbour - centre)

        flux = face(lanes(ext, depth), lanes(kext, depth))
        flux += face(lanes(ext, -depth), lanes(kext, -depth))
        flux += face(pltpu.roll(centre, 1, 0), pltpu.roll(kcentre, 1, 0))
        flux += face(pltpu.roll(centre, rows - 1, 0), pltpu.roll(kcentre, rows - 1, 0))
        flux += face(
            jnp.where(bottom, 0.0, lanes(ext, 1)), jnp.where(bottom, 0.0, lanes(kext, 1))
        )
        flux += face(
            jnp.where(top, 0.0, lanes(ext, -1)), jnp.where(top, 0.0, lanes(kext, -1))
        )
        dx = (xpos - lx_ref[member, step]).astype(jnp.float32)
        dy = ((start + lane) // depth - ly_ref[member, step]).astype(jnp.float32)
        along_x = jnp.exp(-(dx * dx) / beam_spot_width)
        along_y = jnp.exp(-(dy * dy) / beam_spot_width) * (step_dt * laser_power)
        heat = along_x * jnp.where(top, along_y, 0.0)
        return centre + (0.5 * step_dt) * flux + heat

    @pl.loop(0, columns // wide)
    def _(chunk):
        start = pl.multiple_of(chunk * wide, wide)
        umid[:, pl.ds(start + edge, wide)] = advance(ustart, start, 0) * inside

    @pl.loop(0, parts)
    def _(part):
        for sub in range(per_part // wide):
            start = pl.multiple_of(part * per_part + sub * wide, wide)
            done = advance(umid, start, 1)
            out_ref[part, 0, :, sub * wide : (sub + 1) * wide] = done[2 : 2 + planes]


def forecast(field, cond, lx, ly, parts, depth):
    members, planes, columns = field.shape
    first = (lax.axis_index("sa") * planes).astype(jnp.int32).reshape(1)
    total_planes = planes * lax.axis_size("sa")
    low, high = halo(field, "sa", 2)
    cond_low, cond_high = halo(cond, "sa", 2)
    rows = -(-(planes + 4) // 8) * 8
    cond_wide = jnp.pad(
        jnp.concatenate([cond_low, cond, cond_high], axis=0),
        ((0, rows - planes - 4), (128, 128)),
    )
    per_part = columns // parts
    wide = 512 if per_part % 512 == 0 else per_part
    smem = pl.BlockSpec(memory_space=pltpu.SMEM)
    return pl.pallas_call(
        lambda *refs: forecast_kernel(depth, planes, wide, total_planes, *refs),
        grid=(members,),
        in_specs=[
            smem, smem, smem,
            pl.BlockSpec((1, planes, columns), lambda m: (m, 0, 0)),
            pl.BlockSpec((1, 2, columns), lambda m: (m, 0, 0)),
            pl.BlockSpec((1, 2, columns), lambda m: (m, 0, 0)),
            pl.BlockSpec(cond_wide.shape, lambda m: (0, 0)),
        ],
        out_specs=pl.BlockSpec((parts, 1, planes, per_part), lambda m: (0, m, 0, 0)),
        out_shape=jax.ShapeDtypeStruct((parts, members, planes, per_part), jnp.float32),
        scratch_shapes=[pltpu.VMEM((rows, columns + 256), jnp.float32)] * 2,
        name="forecast",
    )(first, lx, ly, field, low, high, cond_wide)


def mix_kernel(gram_ref, proj_ref, out_ref, left, inverse):
    count = gram_ref.shape[0]
    row = lax.broadcasted_iota(jnp.int32, (count, count), 0)
    col = lax.broadcasted_iota(jnp.int32, (count, count), 1)
    eye = jnp.where(row == col, 1.0, 0.0)
    left[...] = eye + gram_ref[...] / (count - 1)
    inverse[...] = eye

    @pl.loop(0, count)
    def _(j):
        whole = left[...]
        pivot_row = left[pl.ds(j, 1), :]
        column = jnp.sum(jnp.where(col == j, whole, 0.0), axis=1, keepdims=True)
        pivot = jnp.sum(jnp.where(col[0:1] == j, pivot_row, 0.0), axis=1, keepdims=True)
        scale = 1.0 / jnp.sqrt(pivot)
        fresh = inverse[pl.ds(j, 1), :] * scale
        below = jnp.where(row[:, 0:1] > j, column * scale, 0.0)
        left[...] = whole - below * (pivot_row * scale)
        inverse[...] = jnp.where(row == j, fresh, inverse[...] - below * fresh)

    root = inverse[...]
    solved = jnp.sum(root * proj_ref[...], axis=1, keepdims=True)
    wmean = jnp.sum(root * solved, axis=0, keepdims=True) / (count - 1)
    mix = root + wmean
    out_ref[...] = mix + (1.0 - jnp.sum(mix, axis=1, keepdims=True)) / count


def join_kernel(parts_ref, out_ref):
    parts, _, _, per_part = parts_ref.shape
    for part in range(parts):
        out_ref[0, :, part * per_part : (part + 1) * per_part] = parts_ref[part, 0]


def per_device(initial_heat_matrix, conductivity, laser_x, laser_y, pixel_cell, observed, obs_var):
    members, planes, columns = initial_heat_matrix.shape
    depth = CELLS_DEPTHWISE
    parts = lax.axis_size("ma")
    per_part = columns // parts
    total_members = members * parts
    states = forecast(initial_heat_matrix, conductivity, laser_x, laser_y, parts, depth)
    gathered = lax.all_to_all(
        states.reshape(total_members, planes, per_part), "ma", split_axis=0, concat_axis=0, tiled=True
    )
    group_rows = per_part // depth
    surface = lax.slice(
        gathered, (0, 0, depth - 1), gathered.shape, (1, 1, depth)
    )
    local_rows = pixel_cell % group_rows
    onehot = (
        local_rows[:, None, :] == jnp.arange(group_rows, dtype=jnp.int32)[None, :, None]
    ).astype(jnp.float32)
    seen = jnp.einsum("kxy,xyj->kxj", surface, onehot, precision=lax.Precision.HIGHEST)
    seen_mean = jnp.mean(seen, axis=0)
    seen_anom = seen - seen_mean[None]
    innovation = observed - seen_mean
    weight = 1.0 / obs_var
    gram_part = jnp.einsum(
        "kxj,lxj->kl", seen_anom * weight[None], seen_anom, precision=lax.Precision.HIGHEST
    )
    proj_part = jnp.einsum(
        "kxj,xj->k", seen_anom, weight * innovation, precision=lax.Precision.HIGHEST
    )
    gram, proj = lax.psum((gram_part, proj_part), ("ma", "sa"))
    mix = pl.pallas_call(
        mix_kernel,
        out_shape=jax.ShapeDtypeStruct(gram.shape, jnp.float32),
        scratch_shapes=[pltpu.VMEM(gram.shape, jnp.float32)] * 2,
        name="mix",
    )(gram, proj.reshape(1, total_members))
    done = jnp.einsum("jxc,kj->kxc", gathered, mix, precision=lax.Precision.HIGHEST)
    back = lax.all_to_all(done, "ma", split_axis=0, concat_axis=0, tiled=True)
    return pl.pallas_call(
        join_kernel,
        grid=(members,),
        in_specs=[pl.BlockSpec((parts, 1, planes, per_part), lambda m: (0, m, 0, 0))],
        out_specs=pl.BlockSpec((1, planes, columns), lambda m: (m, 0, 0)),
        out_shape=jax.ShapeDtypeStruct((members, planes, columns), jnp.float32),
        name="join",
    )(back.reshape(parts, members, planes, per_part))


def solution(mesh):
    placed = (
        P("ma", "sa", None),
        P("sa", None),
        P("ma", None),
        P("ma", None),
        P("sa", "ma"),
        P("sa", "ma"),
        P("sa", "ma"),
    )
    return jax.shard_map(
        per_device, mesh=mesh, in_specs=placed, out_specs=P("ma", "sa", None), check_vma=False
    )
```

time: 2200 us -> 1130 us (0.51)
  local copies, waits for them, and re-layouts: 605 us -> 42.2 us
  other arithmetic: 514 us -> 1.29 us
  Pallas kernels: 0 us -> 165 us
  matrix products: 152 us -> 39.8 us
  loops' own time: 99.2 us -> 0 us
  waiting for transfers between devices: 379 us -> 435 us
    mul x6 -> x0, other arithmetic: 224 us -> none  [the longest x4 223 us: conduct(): kext = cond_ext[None] * (1.0 + alpha_cond * field_ext * field_ext)]
    add x4 -> x0, other arithmetic: 166 us -> none  [the longest x1 165 us: conduct(): return centre + step_dt * (flux + heat)]
    pallas_call x0 -> x3, Pallas kernels: none -> 165 us  [the longest x1 131 us: forecast(): pl.pallas_call(lambda *refs: forecast_kernel(depth, planes, wide, total_p...]
    unnamed x25 -> x18, local copies, waits for them, and re-layouts: 165 us -> 2.68 us
    dynamic_slice x256 -> x0, local copies, waits for them, and re-layouts: 157 us -> none  [the longest x128 81.4 us: column_step(): pivot = jnp.sqrt(lax.dynamic_slice_in_dim(rest, index_j, 1, 0)[0])]
    all_to_all x5 -> x0, local copies, waits for them, and re-layouts: 128 us -> none  [the longest x4 122 us: per_device(): lax.all_to_all(member_states, 'ma', split_axis=2, concat_axis=0, tiled=True)]
    dot_general x259 -> x1, matrix products: 147 us -> 32.6 us  [per_device(): jnp.einsum('jxc,kj->kxc', gathered, mix, precision=lax.Precision.HIGHEST)]
    another operation x2 -> x0, loops' own time: 99.2 us -> none  [the longest x1 94.8 us: lower_factor(): return lax.fori_loop(0, count, column_step, jnp.zeros_like(amat))]
  transfers between devices with their start and end apart: 4 -> 6, of which waited for: 3 -> 2; matrix products, arithmetic and copies ran while one was open for 3% -> 1% of each run, Pallas kernels for 0% -> 0%
where the time goes in v1:
time: 1130 us
  waiting for transfers between devices  435 us (38%)
  blocking collectives  416 us (37%)
  Pallas kernels  165 us (15%)
  local copies, waits for them, and re-layouts  42.2 us (4%)
  matrix products  39.8 us (4%)
  starting transfers between devices  16.9 us (1%)
  between operations  13.6 us (1%)
    all_to_all x1, blocking collectives, per_device(): back = lax.all_to_all(done, 'ma', split_axis=0, concat_axis=0, tiled=True)  369 us
    all_to_all x1, waiting for transfers between devices, per_device(): lax.all_to_all(states.reshape(total_members, planes, per_part), 'ma', spl...  355 us
    pallas_call x1, Pallas kernels, forecast(): pl.pallas_call(lambda *refs: forecast_kernel(depth, planes, wide, total_p...  131 us
    psum x1, waiting for transfers between devices, per_device(): gram, proj = lax.psum((gram_part, proj_part), ('ma', 'sa'))  79.6 us
    psum x1, blocking collectives, per_device(): gram, proj = lax.psum((gram_part, proj_part), ('ma', 'sa'))  46.6 us
    dot_general x1, matrix products, per_device(): jnp.einsum('jxc,kj->kxc', gathered, mix, precision=lax.Precision.HIGHEST)  32.6 us
  transfers between devices with their start and end apart: 6, of which 2 were waited for; matrix products, arithmetic and copies ran while one was open for 1% of the time, Pallas kernels for 0%

profile of v1, /device:TPU:0, one launch (start us, length us, event | category | flops | bytes accessed | tf_op | source)
XLA Modules:
  0.0 1128.9 jit_solution(13350447447581952233)
XLA Ops:
  6.5 1.1 fusion.23
  7.6 2.4 collective-permute-start.2
  10.0 0.0 copy-start.6
  10.0 0.0 copy-start.7
  10.0 0.0 copy-start
  10.1 1.4 collective-permute-start.3
  11.5 5.6 fusion.22
  17.1 1.3 collective-permute-start.1
  18.4 5.8 collective-permute-start
  24.2 0.7 copy.13.refs_1_
  24.9 0.7 copy.14.refs_2_
  25.6 1.3 select_maximum_fusion.refs_6_
  26.9 0.9 copy-done.1
  27.8 0.3 copy-done.2
  28.2 131.0 %forecast.1 = f32[8,16,32,1024]{3,2,1,0:T(8,128)} custom-call(s32[1]{0:T(128)} %bitcast.refs_0_, s32[16,2]{1,0:T(8,128)} %copy.13.refs_1_, s32[16,2]{1,0:T(8,128)} %copy.14.refs_2_, f32[16,32,8192]{2,1,0:T(8,128)} %refs_3_.1, f32[16,2,8192]{2,1,0:T(2,128)} %copy-done.2, f32[16,2,8192]{2,1,0:T(2,128)} %copy-done.1, f32[40,8448]{1,0:T(8,128)} %select_maximum_fusion.refs_6_), custom_call_target="tpu_custom_call" | custom-call | tf_op jit(solution)/shard_map/forecast/pallas_call | solution.py:111
  159.2 6.0 all-to-all-start
  165.1 0.0 all-reduce.3.cloned.1.call-start
  165.2 355.2 %all-to-all-done = f32[128,32,1024]{2,1,0:T(8,128)} async-done(((f32[128,32,1024]{2,1,0:T(8,128)}), f32[128,32,1024]{2,1,0:T(8,128)}, u32[]{:S(2)}, u32[]{:S(2)}) %all-to-all-start) | async-done | bytes 16777248 | tf_op jit(solution)/shard_map/all_to_all | solution.py:168
  520.4 17.6 %slice.19 = f32[128,32,16]{2,1,0:T(8,128)S(1)} slice(f32[128,32,1024]{2,1,0:T(8,128)} %all-to-all-done), slice={[0:128:1], [0:32:1], [63:1024:64]} | slice | bytes 524288 | tf_op jit(solution)/shard_map/slice | solution.py:172
  538.0 0.0 copy-start.4
  538.0 0.0 copy-start.5
  538.0 3.1 fusion.24
  541.1 3.3 fusion.11
  544.4 0.0 all-reduce.3.cloned.1.call-update
  544.5 0.8 convolution_bitcast_fusion
  545.3 46.6 %psum.15.proj_ref = f32[1,128]{1,0:T(1,128)} all-reduce(f32[1,128]{1,0:T(1,128)S(1)} %convolution_bitcast_fusion), channel_id=1, replica_groups=mesh['ma'=8,'sa'=4] {'ma','sa'}, use_global_device_ids=true, to_apply=%region_2.3 | all-reduce | flops 128 | bytes 1024 | tf_op jit(solution)/shard_map/psum | solution.py:190
  591.9 79.6 %all-reduce.3.cloned.1.call-done.gram_ref = f32[128,128]{1,0:T(8,128)} async-done(((f32[128,128]{1,0:T(8,128)}), f32[128,128]{1,0:T(8,128)}) %all-reduce.3.cloned.1.call-update) | async-done | bytes 65552 | tf_op jit(solution)/shard_map/psum | solution.py:190
  671.5 16.4 %mix.1 = f32[128,128]{1,0:T(8,128)} custom-call(f32[128,128]{1,0:T(8,128)} %all-reduce.3.cloned.1.call-done.gram_ref, f32[1,128]{1,0:T(1,128)} %psum.15.proj_ref), custom_call_target="tpu_custom_call" | custom-call | tf_op jit(solution)/shard_map/mix/pallas_call | solution.py:191
  687.9 32.6 %fusion = f32[128,32,1024]{2,0,1:T(8,128)} fusion(f32[128,32,1024]{2,1,0:T(8,128)} %all-to-all-done, f32[128,128]{1,0:T(8,128)} %mix.1), kind=kOutput, calls=%fused_computation | convolution fusion | flops 6442450944 | bytes 33619968 | tf_op jit(solution)/shard_map/jxc,kj->kxc/dot_general | solution.py:197
  720.5 15.2 %copy.17 = f32[128,32,1024]{2,1,0:T(8,128)S(1)} copy(f32[128,32,1024]{2,0,1:T(8,128)} %fusion) | data formatting | bytes 33554432 | tf_op jit(solution)/shard_map/jxc,kj->kxc/dot_general | solution.py:197
  735.7 368.9 %all_to_all.10 = f32[128,32,1024]{2,1,0:T(8,128)} all-to-all(f32[128,32,1024]{2,1,0:T(8,128)S(1)} %copy.17), channel_id=1, replica_groups=mesh['ma'=8,'sa'=4] {'ma'}, dimensions={0} | all-to-all | bytes 33554432 | tf_op jit(solution)/shard_map/all_to_all | solution.py:198
  1104.6 17.4 %join.1 = f32[16,32,8192]{2,1,0:T(8,128)} custom-call(f32[8,16,32,1024]{3,2,1,0:T(8,128)} %bitcast.19), custom_call_target="tpu_custom_call" | custom-call | tf_op jit(solution)/shard_map/join/pallas_call | solution.py:199
  (15 shorter events, 0.1 us)
Async XLA Ops:
  7.6 18.0 %collective-permute-start.2 = (f32[2,8192]{1,0:T(2,128)S(1)}, f32[2,8192]{1,0:T(2,128)S(1)}, u32[]{:S(2)}, u32[]{:S(2)}) collective-permute-start(f32[2,8192]{1,0:T(2,128)S(1)} %get-tuple-element.7), channel_id=1, source_target_pairs={{0,1},{1,2},{2,3},{4,5},{5,6},{6,7},{8,9},{9,10},{10,11},{12,13},{... | collective-permute-start | bytes 196616 | tf_op jit(solution)/shard_map/ppermute | solution.py:22
  10.0 14.2 %copy-start.6 = (s32[16,2]{0,1:T(2,128)S(1)}, s32[16,2]{0,1:T(2,128)}, u32[]{:S(2)}) copy-start(s32[16,2]{0,1:T(2,128)} %param.9) | copy-start | bytes 388
  10.0 14.9 %copy-start.7 = (s32[16,2]{0,1:T(2,128)S(1)}, s32[16,2]{0,1:T(2,128)}, u32[]{:S(2)}) copy-start(s32[16,2]{0,1:T(2,128)} %param.10) | copy-start | bytes 388
  10.0 15.6 %copy-start = (f32[32,8192]{1,0:T(8,128)S(1)}, f32[32,8192]{1,0:T(8,128)}, u32[]{:S(2)}) copy-start(f32[32,8192]{1,0:T(8,128)} %param.8) | copy-start | bytes 3145732
  10.1 15.5 %collective-permute-start.3 = (f32[2,8192]{1,0:T(2,128)S(1)}, f32[2,8192]{1,0:T(2,128)S(1)}, u32[]{:S(2)}, u32[]{:S(2)}) collective-permute-start(f32[2,8192]{1,0:T(2,128)S(1)} %get-tuple-element.8), channel_id=1, source_target_pairs={{1,0},{2,1},{3,2},{5,4},{6,5},{7,6},{9,8},{10,9},{11,10},{13,12},{... | collective-permute-start | bytes 196616 | tf_op jit(solution)/shard_map/ppermute | solution.py:25
  17.1 9.8 collective-permute-start.1
  18.4 8.5 collective-permute-start
  26.9 1.0 copy-start.1
  26.9 1.3 copy-start.2
  159.2 6.0 copy-start.3
  159.2 361.2 %all-to-all-start = ((f32[128,32,1024]{2,1,0:T(8,128)}), f32[128,32,1024]{2,1,0:T(8,128)}, u32[]{:S(2)}, u32[]{:S(2)}) async-start(f32[128,32,1024]{2,1,0:T(8,128)} %bitcast.18), calls=%async_computation | async-start | bytes 33554432 | tf_op jit(solution)/shard_map/all_to_all | solution.py:168
  165.1 506.4 %all-reduce.3.cloned.1.call-start = ((), (), s32[]{:S(2)}) async-start(), calls=%async_computation.2 | async-start | bytes 131072 | tf_op jit(solution)/shard_map/psum | solution.py:190
  538.0 3.1 copy-start.4
  538.0 3.1 copy-start.5
Sparse Core Ops, SparseCore 0:
  544.6 126.8 all-reduce.2
